TPU v7x, 32 devices: a whole 2x2x4 slice. The times are simulated.
32 devices in a mesh: patch: 16 (over z, y, x), frame: 2 (over core).
Axes of the slice: x: 2, y: 2, z: 4, core: 2. Of those that a mesh axis runs over, the one named last changes fastest.
Arguments:
- basis: bfloat16 [3, 4096, 1024], P(None, 'patch'), may hold values from -0.25 to 0.25
- latents: bfloat16 [1024, 1024], P('frame', 'patch'), may hold values from -2 to 2
- rest_pos: float32 [3, 4096], P(None, 'patch'), may hold values from -3 to 3
- triangles: int32 [3, 8192], P(None, 'patch'), may hold values from 0 to 511
- hinges: int32 [4, 6144], P(None, 'patch'), may hold values from 0 to 511
- rest_sq: float32 [3, 8192], P(None, 'patch'), may hold values from 0.5 to 3
- bend_rest: float32 [3, 6144], P(None, 'patch'), may hold values from -5 to 5
- masses: float32 [4096], P('patch'), may hold values from 0.5 to 2
- send_rows: int32 [2, 2048], P(None, 'patch'), may hold values from 0 to 255, as said below
Outputs:
- basis_grad: float32 [3, 4096, 1024], P(None, ('patch', 'frame'))
- latent_grad: float32 [1024, 1024], P('frame', 'patch')
Inputs may be any that keep to these rules, and one draw needn't show every extreme that they name: `send_rows`: within one patch's columns the 256 entries of both rows are distinct own vertex numbers.
All inputs are finite; a program needn't handle non-finite values.
Results may differ from a plain program's by a relative error of at most 0.006.
Values may be sent and summed in bfloat16 or wider, within the bound.
A program may use at most 64 MiB of HBM per device.

v0:
```python
import jax
import jax.numpy as jnp
from jax import lax
from jax.sharding import PartitionSpec as P

MEMBRANE = 5.0
BENDING = 5.0
GRAVITY = 40.0
BF = jnp.bfloat16
F32 = jnp.float32


def shift(block, step):
    n = lax.axis_size("patch")
    return lax.ppermute(block, "patch", [(i, (i + step) % n) for i in range(n)])


def hot(rows, ids):
    iota = lax.broadcasted_iota(jnp.int32, (rows, ids.shape[0]), 0)
    return (iota == ids[None, :]).astype(F32)


def mm(a, b, dims):
    return lax.dot_general(a, b, (dims, ((), ())), preferred_element_type=F32)


def exact(a, b):
    return jnp.dot(a, b, precision=lax.Precision.HIGHEST, preferred_element_type=F32)


def local(basis, latents, rest_pos, triangles, hinges, rest_sq, bend_rest, masses, send_rows):
    vs = basis.shape[1]
    kk = basis.shape[2]
    ff = latents.shape[0]
    halo = send_rows.shape[1]
    nt = triangles.shape[1]
    total = ff * lax.axis_size("frame")
    pos = lax.axis_index("frame")
    lat_t = lax.all_gather(latents.T, "patch", axis=0, tiled=True)
    lat_o = lax.ppermute(lat_t, "frame", [(0, 1), (1, 0)])
    ext = vs + 2 * halo
    ta, tb, tc = (hot(ext, triangles[i]) for i in range(3))
    ha, hb, hc, hd = (hot(ext, hinges[i]) for i in range(4))
    inc = jnp.concatenate([tb - ta, tc - tb, hc + hd - ha - hb], axis=1).astype(BF)
    self32 = hot(vs, send_rows.reshape(-1))
    sel = self32.astype(BF)
    rest_out = exact(rest_pos, self32)
    rest_ext = jnp.concatenate(
        [rest_pos, shift(rest_out[:, halo:], 1), shift(rest_out[:, :halo], -1)], axis=1
    )
    rest_edge = exact(rest_ext, inc.astype(F32))
    rest_edge = rest_edge.at[:, 2 * nt :].add(-bend_rest)
    flat_basis = basis.reshape(3 * vs, kk)
    dec = mm(flat_basis, lat_t, ((1,), (0,))).astype(BF).reshape(3, vs, ff)
    own = jnp.concatenate([dec[0], dec[1], dec[2]], axis=1)
    out = mm(sel, own, ((0,), (0,))).astype(BF)
    dext = jnp.concatenate([own, shift(out[halo:], 1), shift(out[:halo], -1)], axis=0)
    edges = mm(inc, dext, ((0,), (0,)))
    e1 = [edges[:nt, c * ff : (c + 1) * ff] + rest_edge[c, :nt, None] for c in range(3)]
    e2 = [edges[nt : 2 * nt, c * ff : (c + 1) * ff] + rest_edge[c, nt : 2 * nt, None] for c in range(3)]
    hh = [edges[2 * nt :, c * ff : (c + 1) * ff] + rest_edge[c, 2 * nt :, None] for c in range(3)]
    e3 = [-(a + b) for a, b in zip(e1, e2)]
    k = 4.0 * MEMBRANE / total

    def strain(e, r):
        return k * (e[0] * e[0] + e[1] * e[1] + e[2] * e[2] - r[:, None])

    s1, s2, s3 = strain(e1, rest_sq[0]), strain(e2, rest_sq[1]), strain(e3, rest_sq[2])
    u1 = jnp.concatenate([s1 * e1[c] - s3 * e3[c] for c in range(3)], axis=1)
    u2 = jnp.concatenate([s2 * e2[c] - s3 * e3[c] for c in range(3)], axis=1)
    uh = jnp.concatenate(hh, axis=1) * (2.0 * BENDING / total)
    forces = jnp.concatenate([u1, u2, uh], axis=0).astype(BF)
    g = mm(inc, forces, ((1,), (0,)))
    gh = g[vs:].astype(BF)
    back = jnp.concatenate([shift(gh[halo:], 1), shift(gh[:halo], -1)], axis=0)
    owned = g[:vs] + mm(sel, back, ((1,), (0,)))
    owned = owned.at[:, 2 * ff :].add((GRAVITY / total) * masses[:, None])
    adj = owned.astype(BF)
    half = vs // 2
    mine = lax.dynamic_slice_in_dim(adj, pos * half, half, 0)
    other = lax.dynamic_slice_in_dim(adj, (1 - pos) * half, half, 0)
    got = lax.ppermute(other, "frame", [(0, 1), (1, 0)])

    def part(a, lat):
        a3 = jnp.concatenate([a[:, c * ff : (c + 1) * ff] for c in range(3)], axis=0)
        s = lax.optimization_barrier(mm(a3, lat, ((1,), (1,))).astype(BF))
        return s.astype(F32).reshape(3, half, kk)

    basis_grad = part(mine, lat_t) + part(got, lat_o)
    adj3 = jnp.concatenate([adj[:, c * ff : (c + 1) * ff] for c in range(3)], axis=0)
    lg_t = mm(flat_basis, adj3, ((0,), (0,)))
    lg = lax.psum_scatter(lg_t, "patch", scatter_dimension=0, tiled=True)
    return (basis_grad, lg.T)


def solution(mesh):
    return jax.shard_map(
        local,
        mesh=mesh,
        in_specs=(
            P(None, "patch", None),
            P("frame", "patch"),
            P(None, "patch"),
            P(None, "patch"),
            P(None, "patch"),
            P(None, "patch"),
            P(None, "patch"),
            P("patch"),
            P(None, "patch"),
        ),
        out_specs=(P(None, ("patch", "frame"), None), P("frame", "patch")),
        check_vma=False,
    )
```

profile of v0, /device:TPU:0, one launch (start us, length us, event | category | flops | bytes accessed | tf_op | source)
XLA Modules:
  0.0 210.5 jit_solution(3983437293316246059)
XLA Ops:
  7.2 0.0 copy-start
  7.2 0.0 all-gather.2.cloned.1.call-start
  7.2 0.7 all-gather.2.cloned.1.call-update
  7.9 0.0 reduce-scatter.4.cloned.1.call-start
  8.0 0.9 convolution_bitcast_fusion.1
  8.8 3.0 %collective-permute-start.2 = (f32[3,128]{1,0:T(4,128)S(1)}, f32[3,128]{1,0:T(4,128)S(1)}, u32[]{:S(2)}, u32[]{:S(2)}) collective-permute-start(f32[3,128]{1,0:T(4,128)S(1)} %get-tuple-element.80), channel_id=1, source_target_pairs={{0,2},{2,4},{4,6},{6,8},{8,10},{10,12},{12,14},{14,16},{16,18},{18... | collective-permute-start | bytes 4616 | tf_op jit(solution)/shard_map/ppermute | solution.py:15
  11.8 4.1 %collective-permute-start.3 = (f32[3,128]{1,0:T(4,128)S(1)}, f32[3,128]{1,0:T(4,128)S(1)}, u32[]{:S(2)}, u32[]{:S(2)}) collective-permute-start(f32[3,128]{1,0:T(4,128)S(1)} %get-tuple-element.81), channel_id=1, source_target_pairs={{0,30},{2,0},{4,2},{6,4},{8,6},{10,8},{12,10},{14,12},{16,14},{18,... | collective-permute-start | bytes 4616 | tf_op jit(solution)/shard_map/ppermute | solution.py:15
  15.9 0.9 slice_reduce_fusion.6
  16.7 0.8 fusion.81
  17.6 0.4 subtract_convert_fusion.6
  18.0 0.4 fusion.25
  18.4 0.8 fusion.80
  19.2 0.0 collective-permute-done.2
  19.2 0.0 collective-permute-done.3
  19.2 1.4 fusion.57
  20.6 48.0 %all-gather.2.cloned.1.call-done = bf16[1024,512]{1,0:T(8,128)(2,1)} async-done(((bf16[64,512]{1,0:T(8,128)(2,1)}), bf16[1024,512]{1,0:T(8,128)(2,1)}) %all-gather.2.cloned.1.call-update) | async-done | bytes 1048592 | tf_op jit(solution)/shard_map/all_gather | solution.py:39
  68.6 0.0 copy-done
  68.6 0.0 copy-start.2
  68.6 2.3 %convolution_convert_fusion.3 = bf16[768,512]{0,1:T(8,128)(2,1)S(1)} fusion(bf16[768,1024]{1,0:T(8,128)(2,1)S(1)} %bitcast.29, bf16[1024,512]{1,0:T(8,128)(2,1)} %all-gather.2.cloned.1.call-done), kind=kOutput, calls=%fused_computation.35 | convolution fusion | flops 805699584 | bytes 3407872 | tf_op jit(solution)/shard_map/dot_general | solution.py:24
  70.9 0.1 fusion.77
  70.9 0.0 copy-done.2
  70.9 0.0 copy-start.1
  70.9 0.4 convolution_convert_fusion
  71.3 0.1 fusion.76
  71.4 1.5 collective-permute-start
  72.9 4.2 %collective-permute-start.1 = (bf16[128,1536]{0,1:T(8,128)(2,1)S(1)}, bf16[128,1536]{0,1:T(8,128)(2,1)S(1)}, u32[]{:S(2)}, u32[]{:S(2)}) collective-permute-start(bf16[128,1536]{0,1:T(8,128)(2,1)S(1)} %get-tuple-element.61), channel_id=1, source_target_pairs={{0,30},{2,0},{4,2},{6,4},{8,6},{10,8},{12,10},{14,12},{16,14},{18,... | collective-permute-start | bytes 1179656 | tf_op jit(solution)/shard_map/ppermute | solution.py:15
  77.1 0.0 copy-done.1
  77.1 10.6 %collective-permute-done = bf16[128,1536]{0,1:T(8,128)(2,1)S(1)} collective-permute-done((bf16[128,1536]{0,1:T(8,128)(2,1)S(1)}, bf16[128,1536]{0,1:T(8,128)(2,1)S(1)}, u32[]{:S(2)}, u32[]{:S(2)}) %collective-permute-start) | collective-permute-done | bytes 393248 | tf_op jit(solution)/shard_map/ppermute | solution.py:15
  87.7 1.9 collective-permute-done.1
  89.7 2.5 %fusion.15 = f32[1408,1536]{1,0:T(8,128)S(1)} fusion(bf16[128,1536]{0,1:T(8,128)(2,1)S(1)} %collective-permute-done.1, bf16[128,1536]{0,1:T(8,128)(2,1)S(1)} %collective-permute-done, bf16[256,512]{0,1:T(8,128)(2,1)S(1)} %get-tuple-element.63, bf16[256,512]{0,1:T(8,128)(2,1)S(1)} %get-tuple-element.64, bf16[256,512]{0,1:T(8,128)(2,1)S(1)} %get-tuple-element.62, ...), kind=kOutput, calls=%fused_computation.19 | convolution fusion | flops 2226782208 | bytes 11665408 | tf_op jit(solution)/shard_map/dot_general | solution.py:24
  92.1 1.3 subtract_convert_fusion.5
  93.4 0.6 subtract_convert_fusion.2
  94.0 0.2 slice_add_fusion.8
  94.2 0.2 fusion.14
  94.4 0.9 subtract_convert_fusion.4
  95.3 0.0 copy-start.3
  95.3 2.6 %fusion.83 = (bf16[512,1536]{1,0:T(8,128)(2,1)S(1)}, f32[512,1536]{1,0:T(8,128)S(1)}) fusion(bf16[384,1536]{1,0:T(8,128)(2,1)S(1)} %fusion.14, bf16[512,512]{1,0:T(8,128)(2,1)S(1)} %get-tuple-element.47, bf16[512,512]{1,0:T(8,128)(2,1)S(1)} %get-tuple-element.46, bf16[512,512]{1,0:T(8,128)(2,1)S(1)} %get-tuple-element.43, ...), kind=kOutput, calls=%fused_computation.135 | convolution fusion | flops 2249981952 | bytes 10485760 | tf_op jit(solution)/shard_map/dot_general | solution.py:24
  97.9 0.1 fusion.74
  98.0 0.6 collective-permute-start.4
  98.6 5.1 %collective-permute-start.5 = (bf16[128,1536]{1,0:T(8,128)(2,1)S(1)}, bf16[128,1536]{1,0:T(8,128)(2,1)S(1)}, u32[]{:S(2)}, u32[]{:S(2)}) collective-permute-start(bf16[128,1536]{1,0:T(8,128)(2,1)S(1)} %get-tuple-element.53), channel_id=1, source_target_pairs={{0,30},{2,0},{4,2},{6,4},{8,6},{10,8},{12,10},{14,12},{16,14},{18,... | collective-permute-start | bytes 1179656 | tf_op jit(solution)/shard_map/ppermute | solution.py:15
  103.7 0.0 copy-done.3
  103.7 9.6 %collective-permute-done.4 = bf16[128,1536]{1,0:T(8,128)(2,1)S(1)} collective-permute-done((bf16[128,1536]{1,0:T(8,128)(2,1)S(1)}, bf16[128,1536]{1,0:T(8,128)(2,1)S(1)}, u32[]{:S(2)}, u32[]{:S(2)}) %collective-permute-start.4) | collective-permute-done | bytes 393248 | tf_op jit(solution)/shard_map/ppermute | solution.py:15
  113.3 2.1 collective-permute-done.5
  115.4 0.4 convolution_add_fusion
  115.8 0.1 fusion.43
  115.9 0.1 convert_element_type.63
  116.0 0.1 fusion.75
  116.0 2.3 %convolution_bitcast_fusion = f32[1024,512]{0,1:T(8,128)} fusion(bf16[768,1024]{1,0:T(8,128)(2,1)S(1)} %bitcast.30, bf16[256,512]{1,0:T(8,128)(2,1)S(1)} %get-tuple-element.55, bf16[256,512]{1,0:T(8,128)(2,1)S(1)} %get-tuple-element.56, bf16[256,512]{1,0:T(8,128)(2,1)S(1)} %get-tuple-element.54), kind=kOutput, calls=%fused_computation.18 | convolution fusion | flops 807665664 | bytes 4456448 | tf_op jit(solution)/shard_map/dot_general | solution.py:24
  118.4 2.9 %copy.16 = f32[1024,512]{1,0:T(8,128)} copy(f32[1024,512]{0,1:T(8,128)} %convolution_bitcast_fusion) | data formatting | bytes 4194304
  121.3 0.0 reduce-scatter.4.cloned.1.call-update
  121.3 0.1 collective-permute-start.7
  121.5 0.5 collective-permute-start.6
  122.0 1.8 convolution_convert_fusion.2
  123.9 0.9 collective-permute-done.6
  124.9 0.0 collective-permute-done.7
  124.9 1.8 convolution_convert_fusion.1
  126.7 1.4 convert_add_fusion
  128.2 75.5 %reduce-scatter.4.cloned.1.call-done = f32[64,512]{1,0:T(8,128)} async-done(((f32[1024,512]{1,0:T(8,128)}), f32[64,512]{1,0:T(8,128)}) %reduce-scatter.4.cloned.1.call-update) | async-done | bytes 131088
  (8 shorter events, 0.1 us)
Async XLA Ops:
  7.2 61.4 %copy-start = (bf16[3,256,1024]{2,1,0:T(8,128)(2,1)S(1)}, bf16[3,256,1024]{2,1,0:T(8,128)(2,1)}, u32[]{:S(2)}) copy-start(bf16[3,256,1024]{2,1,0:T(8,128)(2,1)} %param.13) | copy-start | bytes 4718596
  7.2 61.4 %all-gather.2.cloned.1.call-start = ((), (), s32[]{:S(2)}) async-start(), calls=%async_computation.1 | async-start | bytes 1114112 | tf_op jit(solution)/shard_map/all_gather | solution.py:39
  7.9 195.7 %reduce-scatter.4.cloned.1.call-start = ((), (), s32[]{:S(2)}) async-start(), calls=%async_computation.2 | async-start | bytes 2228224
  8.8 10.4 %collective-permute-start.2 = (f32[3,128]{1,0:T(4,128)S(1)}, f32[3,128]{1,0:T(4,128)S(1)}, u32[]{:S(2)}, u32[]{:S(2)}) collective-permute-start(f32[3,128]{1,0:T(4,128)S(1)} %get-tuple-element.80), channel_id=1, source_target_pairs={{0,2},{2,4},{4,6},{6,8},{8,10},{10,12},{12,14},{14,16},{16,18},{18... | collective-permute-start | bytes 4616 | tf_op jit(solution)/shard_map/ppermute | solution.py:15
  11.8 7.4 %collective-permute-start.3 = (f32[3,128]{1,0:T(4,128)S(1)}, f32[3,128]{1,0:T(4,128)S(1)}, u32[]{:S(2)}, u32[]{:S(2)}) collective-permute-start(f32[3,128]{1,0:T(4,128)S(1)} %get-tuple-element.81), channel_id=1, source_target_pairs={{0,30},{2,0},{4,2},{6,4},{8,6},{10,8},{12,10},{14,12},{16,14},{18,... | collective-permute-start | bytes 4616 | tf_op jit(solution)/shard_map/ppermute | solution.py:15
  68.6 2.3 %copy-start.2 = (s32[2,128]{1,0:T(2,128)S(1)}, s32[2,128]{1,0:T(2,128)}, u32[]{:S(2)}) copy-start(s32[2,128]{1,0:T(2,128)} %param.21) | copy-start | bytes 3076
  70.9 6.1 %copy-start.1 = (f32[3,384]{1,0:T(4,128)S(1)}, f32[3,384]{1,0:T(4,128)}, u32[]{:S(2)}) copy-start(f32[3,384]{1,0:T(4,128)} %param.19) | copy-start | bytes 13828
  71.4 16.3 %collective-permute-start = (bf16[128,1536]{0,1:T(8,128)(2,1)S(1)}, bf16[128,1536]{0,1:T(8,128)(2,1)S(1)}, u32[]{:S(2)}, u32[]{:S(2)}) collective-permute-start(bf16[128,1536]{0,1:T(8,128)(2,1)S(1)} %get-tuple-element.60), channel_id=1, source_target_pairs={{0,2},{2,4},{4,6},{6,8},{8,10},{10,12},{12,14},{14,16},{16,18},{18... | collective-permute-start | bytes 1179656 | tf_op jit(solution)/shard_map/ppermute | solution.py:15
  72.9 16.8 %collective-permute-start.1 = (bf16[128,1536]{0,1:T(8,128)(2,1)S(1)}, bf16[128,1536]{0,1:T(8,128)(2,1)S(1)}, u32[]{:S(2)}, u32[]{:S(2)}) collective-permute-start(bf16[128,1536]{0,1:T(8,128)(2,1)S(1)} %get-tuple-element.61), channel_id=1, source_target_pairs={{0,30},{2,0},{4,2},{6,4},{8,6},{10,8},{12,10},{14,12},{16,14},{18,... | collective-permute-start | bytes 1179656 | tf_op jit(solution)/shard_map/ppermute | solution.py:15
  95.3 8.4 %copy-start.3 = (f32[256]{0:T(256)S(1)}, f32[256]{0:T(256)}, u32[]{:S(2)}) copy-start(f32[256]{0:T(256)} %param.20) | copy-start | bytes 3076
  98.0 15.3 %collective-permute-start.4 = (bf16[128,1536]{1,0:T(8,128)(2,1)S(1)}, bf16[128,1536]{1,0:T(8,128)(2,1)S(1)}, u32[]{:S(2)}, u32[]{:S(2)}) collective-permute-start(bf16[128,1536]{1,0:T(8,128)(2,1)S(1)} %get-tuple-element.52), channel_id=1, source_target_pairs={{0,2},{2,4},{4,6},{6,8},{8,10},{10,12},{12,14},{14,16},{16,18},{18... | collective-permute-start | bytes 1179656 | tf_op jit(solution)/shard_map/ppermute | solution.py:15
  98.6 16.8 %collective-permute-start.5 = (bf16[128,1536]{1,0:T(8,128)(2,1)S(1)}, bf16[128,1536]{1,0:T(8,128)(2,1)S(1)}, u32[]{:S(2)}, u32[]{:S(2)}) collective-permute-start(bf16[128,1536]{1,0:T(8,128)(2,1)S(1)} %get-tuple-element.53), channel_id=1, source_target_pairs={{0,30},{2,0},{4,2},{6,4},{8,6},{10,8},{12,10},{14,12},{16,14},{18,... | collective-permute-start | bytes 1179656 | tf_op jit(solution)/shard_map/ppermute | solution.py:15
  121.3 3.5 %collective-permute-start.7 = (bf16[1024,512]{1,0:T(8,128)(2,1)}, bf16[1024,512]{1,0:T(8,128)(2,1)}, u32[]{:S(2)}, u32[]{:S(2)}) collective-permute-start(bf16[1024,512]{1,0:T(8,128)(2,1)} %all-gather.2.cloned.1.call-done), channel_id=1, source_target_pairs={{0,1},{1,0},{2,3},{3,2},{4,5},{5,4},{6,7},{7,6},{8,9},{9,8},{10,11... | collective-permute-start | bytes 3145736 | tf_op jit(solution)/shard_map/ppermute | solution.py:40
  121.5 3.4 %collective-permute-start.6 = (bf16[128,1536]{1,0:T(8,128)(2,1)S(1)}, bf16[128,1536]{1,0:T(8,128)(2,1)S(1)}, u32[]{:S(2)}, u32[]{:S(2)}) collective-permute-start(bf16[128,1536]{1,0:T(8,128)(2,1)S(1)} %constant_dynamic-slice_fusion.1), channel_id=1, source_target_pairs={{0,1},{1,0},{2,3},{3,2},{4,5},{5,4},{6,7},{7,6},{8,9},{9,8},{10,11... | collective-permute-start | bytes 1179656 | tf_op jit(solution)/shard_map/ppermute | solution.py:82
Sparse Core Ops, SparseCore 0:
  10.7 57.7 all-gather.1
  121.4 82.1 reduce-scatter.3
where the time goes:
time: 211 us; the launch traced here: 210 us
  waiting for transfers between devices  149 us (71%)
  starting transfers between devices  19.1 us (9%)
  matrix products  16.3 us (8%)
  between operations  14.3 us (7%)
  local copies, waits for them, and re-layouts  5.8 us (3%)
  other arithmetic  5.62 us (3%)
    unnamed x3, waiting for transfers between devices  76.2 us
    all_gather x1, waiting for transfers between devices, local(): lat_t = lax.all_gather(latents.T, 'patch', axis=0, tiled=True)  48 us
    ppermute x6, waiting for transfers between devices, shift(): return lax.ppermute(block, 'patch', [(i, (i + step) % n) for i in range(n)])  24.3 us
    ppermute x6, starting transfers between devices, shift(): return lax.ppermute(block, 'patch', [(i, (i + step) % n) for i in range(n)])  18.4 us
    dot_general x8, matrix products, mm(): return lax.dot_general(a, b, (dims, ((), ())), preferred_element_type=F32)  14.1 us
  transfers between devices with their start and end apart: 10, of which 7 were waited for; matrix products, arithmetic and copies ran while one was open for 5% of the time, Pallas kernels for 0%

commit v1 on v0

--- a/solution.py
+++ b/solution.py
@@ -1,6 +1,10 @@
+import functools
+
 import jax
 import jax.numpy as jnp
 from jax import lax
+from jax.experimental import pallas as pl
+from jax.experimental.pallas import tpu as pltpu
 from jax.sharding import PartitionSpec as P
 
 MEMBRANE = 5.0
@@ -26,6 +30,174 @@
 
 def exact(a, b):
     return jnp.dot(a, b, precision=lax.Precision.HIGHEST, preferred_element_type=F32)
+
+
+PLANE = 4
+MESH_ID = pl.DeviceIdType.MESH
+DMA = pltpu.SemaphoreType.DMA
+
+
+def places(n):
+    p = lax.axis_index("patch")
+    xnb = p + 1 - 2 * (p % 2)
+    ynb = p + 2 - 4 * ((p // 2) % 2)
+    return p, p // PLANE, p % PLANE, xnb, ynb
+
+
+def greet(peers):
+    bar = pltpu.get_barrier_semaphore()
+    for q in peers:
+        pl.semaphore_signal(bar, inc=1, device_id={"patch": q}, device_id_type=MESH_ID)
+    pl.semaphore_wait(bar, len(peers))
+
+
+def send(src, dst, ss, rs, q):
+    return pltpu.make_async_remote_copy(
+        src_ref=src, dst_ref=dst, send_sem=ss, recv_sem=rs,
+        device_id={"patch": q}, device_id_type=MESH_ID,
+    )
+
+
+def gather_kernel(n, w, x_ref, o_ref, zs, zr, xs, xr, ys, yr, rs, rr):
+    hi = n // PLANE
+    p, h, lo, xnb, ynb = places(n)
+    lox, loy = xnb % PLANE, ynb % PLANE
+
+    def rows(hh, ll):
+        return o_ref.at[pl.ds(pl.multiple_of((hh * PLANE + ll) * w, w), w)]
+
+    zpeer = [((h + j) % hi) * PLANE + lo for j in range(hi)]
+    greet(zpeer[1:] + [xnb, ynb])
+    order = sorted(range(1, hi), key=lambda j: min(j, hi - j))
+    mine = rows(h, lo)
+    zc = {j: send(x_ref, mine, zs.at[j], zr.at[j], zpeer[j]) for j in order}
+    xc, yc, rc = {}, {}, {}
+    xc[0] = send(x_ref, mine, xs.at[0], xr.at[0], xnb)
+    yc[0] = send(x_ref, mine, ys.at[0], yr.at[0], ynb)
+    xc[0].start()
+    yc[0].start()
+    for j in reversed(order):
+        zc[j].start()
+    mine[...] = x_ref[...]
+
+    def relay(j):
+        hh = (h + hi - j) % hi
+        if j % 2 == 0:
+            xc[j].wait_recv()
+            part = rows(hh, lox)
+            rc[j] = send(part, part, rs.at[j], rr.at[j], ynb)
+        else:
+            yc[j].wait_recv()
+            part = rows(hh, loy)
+            rc[j] = send(part, part, rs.at[j], rr.at[j], xnb)
+        rc[j].start()
+
+    last = 0
+    for j in order:
+        zc[j].wait_recv()
+        part = rows((h + hi - j) % hi, lo)
+        xc[j] = send(part, part, xs.at[j], xr.at[j], xnb)
+        yc[j] = send(part, part, ys.at[j], yr.at[j], ynb)
+        xc[j].start()
+        yc[j].start()
+        relay(last)
+        last = j
+    relay(last)
+    for j in range(hi):
+        if j % 2 == 0:
+            yc[j].wait_recv()
+        else:
+            xc[j].wait_recv()
+        rc[j].wait_recv()
+    for j in range(hi):
+        if j:
+            zc[j].wait_send()
+        xc[j].wait_send()
+        yc[j].wait_send()
+        rc[j].wait_send()
+
+
+def gather_all(x, n):
+    w, f = x.shape
+    hi = n // PLANE
+    return pl.pallas_call(
+        functools.partial(gather_kernel, n, w),
+        out_shape=jax.ShapeDtypeStruct((n * w, f), x.dtype),
+        in_specs=[pl.BlockSpec(memory_space=pltpu.VMEM)],
+        out_specs=pl.BlockSpec(memory_space=pltpu.VMEM),
+        scratch_shapes=[DMA((hi,))] * 8,
+        compiler_params=pltpu.CompilerParams(collective_id=0, has_side_effects=True),
+    )(x)
+
+
+def scatter_kernel(
+    n, w, g_ref, o_ref, rl, sb, cx, cy, zb, zl, ls, lr, xs, xr, ys, yr, zs, zr
+):
+    hi = n // PLANE
+    p, h, lo, xnb, ynb = places(n)
+    lox, loy = xnb % PLANE, ynb % PLANE
+    lod = PLANE - 1 - lo
+
+    def rows(j, ll):
+        hh = (h + j) % hi
+        return g_ref.at[pl.ds(pl.multiple_of((hh * PLANE + ll) * w, w), w)]
+
+    zpeer = [((h + j) % hi) * PLANE + lo for j in range(hi)]
+    greet(zpeer[1:] + [xnb, ynb])
+    order = sorted(range(1, hi), key=lambda j: -min(j, hi - j)) + [0]
+    lc, xc, yc, zc = {}, {}, {}, {}
+    for j in order:
+        lc[j] = send(rows(j, lod), rl.at[j], ls.at[j], lr.at[j], xnb if j % 2 == 0 else ynb)
+        lc[j].start()
+    for j in order:
+        if j % 2 == 0:
+            xc[j] = send(rows(j, lox), cx.at[j], xs.at[j], xr.at[j], xnb)
+            xc[j].start()
+        else:
+            yc[j] = send(rows(j, loy), cy.at[j], ys.at[j], yr.at[j], ynb)
+            yc[j].start()
+    for j in order:
+        lc[j].wait_recv()
+        own = rows(j, loy if j % 2 == 0 else lox)
+        sb[j] = (own[...].astype(F32) + rl[j].astype(F32)).astype(BF)
+        if j % 2 == 0:
+            yc[j] = send(sb.at[j], cy.at[j], ys.at[j], yr.at[j], ynb)
+            yc[j].start()
+        else:
+            xc[j] = send(sb.at[j], cx.at[j], xs.at[j], xr.at[j], xnb)
+            xc[j].start()
+    for j in order:
+        xc[j].wait_recv()
+        yc[j].wait_recv()
+        s = rows(j, lo)[...].astype(F32) + cx[j].astype(F32) + cy[j].astype(F32)
+        if j:
+            zb[j] = s.astype(BF)
+            zc[j] = send(zb.at[j], zl.at[j], zs.at[j], zr.at[j], zpeer[j])
+            zc[j].start()
+    for j in reversed(order[:-1]):
+        zc[j].wait_recv()
+        s = s + zl[j].astype(F32)
+    o_ref[...] = s
+    for j in order:
+        lc[j].wait_send()
+        xc[j].wait_send()
+        yc[j].wait_send()
+        if j:
+            zc[j].wait_send()
+
+
+def scatter_sum(g, n):
+    f = g.shape[1]
+    w = g.shape[0] // n
+    hi = n // PLANE
+    return pl.pallas_call(
+        functools.partial(scatter_kernel, n, w),
+        out_shape=jax.ShapeDtypeStruct((w, f), F32),
+        in_specs=[pl.BlockSpec(memory_space=pltpu.VMEM)],
+        out_specs=pl.BlockSpec(memory_space=pltpu.VMEM),
+        scratch_shapes=[pltpu.VMEM((hi, w, f), BF)] * 6 + [DMA((hi,))] * 8,
+        compiler_params=pltpu.CompilerParams(collective_id=1, has_side_effects=True),
+    )(g)
 
 
 def local(basis, latents, rest_pos, triangles, hinges, rest_sq, bend_rest, masses, send_rows):
@@ -36,7 +208,8 @@
     nt = triangles.shape[1]
     total = ff * lax.axis_size("frame")
     pos = lax.axis_index("frame")
-    lat_t = lax.all_gather(latents.T, "patch", axis=0, tiled=True)
+    n = lax.axis_size("patch")
+    lat_t = gather_all(latents.T, n)
     lat_o = lax.ppermute(lat_t, "frame", [(0, 1), (1, 0)])
     ext = vs + 2 * halo
     ta, tb, tc = (hot(ext, triangles[i]) for i in range(3))
@@ -88,8 +261,8 @@
 
     basis_grad = part(mine, lat_t) + part(got, lat_o)
     adj3 = jnp.concatenate([adj[:, c * ff : (c + 1) * ff] for c in range(3)], axis=0)
-    lg_t = mm(flat_basis, adj3, ((0,), (0,)))
-    lg = lax.psum_scatter(lg_t, "patch", scatter_dimension=0, tiled=True)
+    lg_t = mm(flat_basis, adj3, ((0,), (0,))).astype(BF)
+    lg = scatter_sum(lg_t, n)
     return (basis_grad, lg.T)
 
 

time: 211 us -> 108 us (0.51)
  waiting for transfers between devices: 149 us -> 18.1 us
  Pallas kernels: 0 us -> 45.3 us
  between operations: 14.3 us -> 0.91 us
    unnamed x3 -> x0, waiting for transfers between devices: 76.2 us -> none
    all_gather x1 -> x0, waiting for transfers between devices: 48 us -> none  [local(): lat_t = lax.all_gather(latents.T, 'patch', axis=0, tiled=True)]
    pallas_call x0 -> x2, Pallas kernels: none -> 45.3 us  [the longest x1 25.1 us: gather_all(): pl.pallas_call(functools.partial(gather_kernel, n, w), out_shape=jax.Shap...]
    ppermute x6, waiting for transfers between devices: 24.3 us -> 18.1 us  [shift(): return lax.ppermute(block, 'patch', [(i, (i + step) % n) for i in range(n)])]
  transfers between devices with their start and end apart: 10 -> 8, of which waited for: 7 -> 4; matrix products, arithmetic and copies ran while one was open for 5% -> 8% of each run, Pallas kernels for 0% -> 19%
where the time goes in v1:
time: 108 us
  Pallas kernels  45.3 us (42%)
  waiting for transfers between devices  18.1 us (17%)
  starting transfers between devices  17 us (16%)
  matrix products  16.4 us (15%)
  other arithmetic  5.63 us (5%)
  local copies, waits for them, and re-layouts  4.42 us (4%)
    pallas_call x1, Pallas kernels, gather_all(): pl.pallas_call(functools.partial(gather_kernel, n, w), out_shape=jax.Shap...  25.1 us
    pallas_call x1, Pallas kernels, scatter_sum(): pl.pallas_call(functools.partial(scatter_kernel, n, w), out_shape=jax.Sha...  20.2 us
    ppermute x6, waiting for transfers between devices, shift(): return lax.ppermute(block, 'patch', [(i, (i + step) % n) for i in range(n)])  18.1 us
    ppermute x6, starting transfers between devices, shift(): return lax.ppermute(block, 'patch', [(i, (i + step) % n) for i in range(n)])  17 us
    dot_general x8, matrix products, mm(): return lax.dot_general(a, b, (dims, ((), ())), preferred_element_type=F32)  15.5 us
    another operation x6, other arithmetic  3.76 us
  transfers between devices with their start and end apart: 8, of which 4 were waited for; matrix products, arithmetic and copies ran while one was open for 8% of the time, Pallas kernels for 19%

profile of v1, /device:TPU:0, one launch (start us, length us, event | category | flops | bytes accessed | tf_op | source)
XLA Modules:
  0.0 107.7 jit_solution(2893642028453221869)
XLA Ops:
  0.6 0.0 copy-start
  0.6 25.1 %shard_map.104 = bf16[1024,512]{1,0:T(8,128)(2,1)} custom-call(bf16[64,512]{1,0:T(8,128)(2,1)} %bitcast.31), custom_call_target="tpu_custom_call" | custom-call | tf_op jit(solution)/shard_map/pallas_call | solution.py:123
  25.8 0.0 copy-done
  25.8 2.3 %convolution_convert_fusion.4 = bf16[768,512]{0,1:T(8,128)(2,1)S(1)} fusion(bf16[768,1024]{1,0:T(8,128)(2,1)S(1)} %bitcast.27, bf16[1024,512]{1,0:T(8,128)(2,1)} %shard_map.104), kind=kOutput, calls=%fused_computation.35 | convolution fusion | flops 805699584 | bytes 3407872 | tf_op jit(solution)/shard_map/dot_general | solution.py:28
  28.0 0.0 copy-start.7
  28.1 0.1 fusion.78
  28.1 0.6 copy-done.7
  28.7 0.0 copy-start.9
  28.7 0.0 copy-start.3
  28.7 0.0 copy-start.5
  28.7 0.4 convolution_convert_fusion
  29.1 0.0 copy-start.6
  29.1 0.1 fusion.77
  29.2 0.5 collective-permute-start
  29.7 5.2 %collective-permute-start.1 = (bf16[128,1536]{0,1:T(8,128)(2,1)S(1)}, bf16[128,1536]{0,1:T(8,128)(2,1)S(1)}, u32[]{:S(2)}, u32[]{:S(2)}) collective-permute-start(bf16[128,1536]{0,1:T(8,128)(2,1)S(1)} %get-tuple-element.57), channel_id=1, source_target_pairs={{0,30},{2,0},{4,2},{6,4},{8,6},{10,8},{12,10},{14,12},{16,14},{18,... | collective-permute-start | bytes 1179656 | tf_op jit(solution)/shard_map/ppermute | solution.py:19
  34.9 0.0 copy-done.9
  34.9 0.1 convolution_bitcast_fusion
  35.0 0.0 collective-permute-start.2
  35.0 5.7 %collective-permute-start.3 = (f32[3,128]{1,0:T(4,128)S(1)}, f32[3,128]{1,0:T(4,128)S(1)}, u32[]{:S(2)}, u32[]{:S(2)}) collective-permute-start(f32[3,128]{1,0:T(4,128)S(1)} %get-tuple-element.77), channel_id=1, source_target_pairs={{0,30},{2,0},{4,2},{6,4},{8,6},{10,8},{12,10},{14,12},{16,14},{18,... | collective-permute-start | bytes 4616 | tf_op jit(solution)/shard_map/ppermute | solution.py:19
  40.7 0.0 copy-done.3
  40.7 0.0 copy-done.5
  40.7 0.4 fusion.26
  41.2 0.4 subtract_convert_fusion.6
  41.6 0.0 copy-done.6
  41.6 2.6 %collective-permute-done.2 = f32[3,128]{1,0:T(4,128)S(1)} collective-permute-done((f32[3,128]{1,0:T(4,128)S(1)}, f32[3,128]{1,0:T(4,128)S(1)}, u32[]{:S(2)}, u32[]{:S(2)}) %collective-permute-start.2) | collective-permute-done | bytes 1568 | tf_op jit(solution)/shard_map/ppermute | solution.py:19
  44.2 1.9 %collective-permute-done.3 = f32[3,128]{1,0:T(4,128)S(1)} collective-permute-done((f32[3,128]{1,0:T(4,128)S(1)}, f32[3,128]{1,0:T(4,128)S(1)}, u32[]{:S(2)}, u32[]{:S(2)}) %collective-permute-start.3) | collective-permute-done | bytes 1568 | tf_op jit(solution)/shard_map/ppermute | solution.py:19
  46.1 0.0 copy-start.4
  46.1 0.7 fusion.58
  46.7 0.0 copy-done.4
  46.8 0.0 collective-permute-done
  46.8 0.0 collective-permute-done.1
  46.9 2.5 %fusion.15 = f32[1408,1536]{1,0:T(8,128)S(1)} fusion(bf16[128,1536]{0,1:T(8,128)(2,1)S(1)} %collective-permute-done.1, bf16[128,1536]{0,1:T(8,128)(2,1)S(1)} %collective-permute-done, bf16[256,512]{0,1:T(8,128)(2,1)S(1)} %get-tuple-element.59, bf16[256,512]{0,1:T(8,128)(2,1)S(1)} %get-tuple-element.60, bf16[256,512]{0,1:T(8,128)(2,1)S(1)} %get-tuple-element.58, ...), kind=kOutput, calls=%fused_computation.18 | convolution fusion | flops 2226782208 | bytes 11665408 | tf_op jit(solution)/shard_map/dot_general | solution.py:28
  49.3 1.3 %subtract_convert_fusion.5 = (bf16[512,512]{1,0:T(8,128)(2,1)S(1)}, f32[512,512]{1,0:T(8,128)S(1)}, f32[512,512]{1,0:T(8,128)S(1)}, f32[512,512]{1,0:T(8,128)S(1...) fusion(f32[1408,1536]{1,0:T(8,128)S(1)} %fusion.15, f32[512]{0:T(512)S(1)} %bitcast.44, f32[512]{0:T(512)S(1)} %bitcast.46, ...), kind=kLoop, calls=%fused_computation.54 | loop fusion | flops 7340032 | bytes 12075008 | tf_op jit(solution)/shard_map/convert.7
  50.6 0.6 subtract_convert_fusion.2
  51.2 0.2 slice_add_fusion.8
  51.4 0.2 fusion.14
  51.6 0.9 subtract_convert_fusion.4
  52.5 4.2 %fusion.84 = (bf16[512,1536]{1,0:T(8,128)(2,1)S(1)}, f32[512,1536]{1,0:T(8,128)}) fusion(bf16[384,1536]{1,0:T(8,128)(2,1)S(1)} %fusion.14, bf16[512,512]{1,0:T(8,128)(2,1)S(1)} %get-tuple-element.43, bf16[512,512]{1,0:T(8,128)(2,1)S(1)} %get-tuple-element.42, bf16[512,512]{1,0:T(8,128)(2,1)S(1)} %get-tuple-element.39, ...), kind=kOutput, calls=%fused_computation.136 | convolution fusion | flops 2249981952 | bytes 10485760 | tf_op jit(solution)/shard_map/dot_general | solution.py:28
  56.7 0.0 copy-start.1
  56.8 0.9 fusion.75
  57.7 0.7 collective-permute-start.4
  58.4 5.0 %collective-permute-start.5 = (bf16[128,1536]{1,0:T(8,128)(2,1)}, bf16[128,1536]{1,0:T(8,128)(2,1)S(1)}, u32[]{:S(2)}, u32[]{:S(2)}) collective-permute-start(bf16[128,1536]{1,0:T(8,128)(2,1)} %get-tuple-element.49), channel_id=1, source_target_pairs={{0,30},{2,0},{4,2},{6,4},{8,6},{10,8},{12,10},{14,12},{16,14},{18,... | collective-permute-start | bytes 1179656 | tf_op jit(solution)/shard_map/ppermute | solution.py:19
  63.3 0.0 copy-done.1
  63.3 0.0 collective-permute-start.7
  63.3 0.0 copy-done.8
  63.3 8.9 %collective-permute-done.4 = bf16[128,1536]{1,0:T(8,128)(2,1)S(1)} collective-permute-done((bf16[128,1536]{1,0:T(8,128)(2,1)}, bf16[128,1536]{1,0:T(8,128)(2,1)S(1)}, u32[]{:S(2)}, u32[]{:S(2)}) %collective-permute-start.4) | collective-permute-done | bytes 393248 | tf_op jit(solution)/shard_map/ppermute | solution.py:19
  72.3 4.7 %collective-permute-done.5 = bf16[128,1536]{1,0:T(8,128)(2,1)S(1)} collective-permute-done((bf16[128,1536]{1,0:T(8,128)(2,1)}, bf16[128,1536]{1,0:T(8,128)(2,1)S(1)}, u32[]{:S(2)}, u32[]{:S(2)}) %collective-permute-start.5) | collective-permute-done | bytes 393248 | tf_op jit(solution)/shard_map/ppermute | solution.py:19
  77.0 1.8 %convolution_add_fusion = f32[256,1536]{1,0:T(8,128)S(1)} fusion(f32[512,1536]{1,0:T(8,128)} %get-tuple-element.81, bf16[128,1536]{1,0:T(8,128)(2,1)S(1)} %collective-permute-done.5, bf16[128,1536]{1,0:T(8,128)(2,1)S(1)} %collective-permute-done.4, s32[256]{0:T(256)S(1)} %bitcast.53), kind=kOutput, calls=%fused_computation.14 | convolution fusion | flops 203489280 | bytes 3933184 | tf_op jit(solution)/shard_map/dot_general | solution.py:28
  78.8 0.1 fusion.44
  78.9 0.1 convert_element_type.68
  79.0 0.1 fusion.76
  79.0 0.8 constant_dynamic-slice_fusion.1
  79.8 0.0 collective-permute-start.6
  79.8 2.0 %fusion.25.g_ref = bf16[1024,512]{1,0:T(8,128)(2,1)} fusion(bf16[768,1024]{1,0:T(8,128)(2,1)S(1)} %bitcast.28, bf16[256,512]{1,0:T(8,128)(2,1)S(1)} %get-tuple-element.51, bf16[256,512]{1,0:T(8,128)(2,1)S(1)} %get-tuple-element.52, bf16[256,512]{1,0:T(8,128)(2,1)S(1)} %get-tuple-element.50), kind=kOutput, calls=%fused_computation.36 | convolution fusion | flops 808189952 | bytes 3407872 | tf_op jit(solution)/shard_map/dot_general | solution.py:28
  81.8 20.2 %shard_map.105 = f32[64,512]{1,0:T(8,128)} custom-call(bf16[1024,512]{1,0:T(8,128)(2,1)} %fusion.25.g_ref), custom_call_target="tpu_custom_call" | custom-call | tf_op jit(solution)/shard_map/pallas_call | solution.py:193
  102.1 0.6 convolution_convert_fusion.3
  102.7 0.0 collective-permute-done.6
  102.7 1.1 fusion.79
  103.8 0.0 collective-permute-done.7
  103.8 1.8 %convolution_convert_fusion.2 = bf16[384,1024]{1,0:T(8,128)(2,1)S(1)} fusion(bf16[1024,512]{1,0:T(8,128)(2,1)} %collective-permute-done.7, bf16[128,512]{1,0:T(8,128)(2,1)S(1)} %get-tuple-element.62, bf16[128,512]{1,0:T(8,128)(2,1)S(1)} %get-tuple-element.63, bf16[128,512]{1,0:T(8,128)(2,1)S(1)} %get-tuple-element.61), kind=kOutput, calls=%fused_computation.33 | convolution fusion | flops 404226048 | bytes 2228224 | tf_op jit(solution)/shard_map/dot_general | solution.py:28
  105.6 0.0 copy-start.2
  105.7 1.4 %convert_add_fusion = f32[384,1024]{1,0:T(8,128)} fusion(bf16[384,1024]{1,0:T(8,128)(2,1)S(1)} %convolution_convert_fusion.2, bf16[384,1024]{1,0:T(8,128)(2,1)S(1)} %convolution_convert_fusion.3), kind=kLoop, calls=%fused_computation.28 | loop fusion | flops 1179648 | bytes 3145728 | tf_op jit(solution)/shard_map/add | solution.py:262
  107.1 0.0 copy-done.2
  107.1 0.7 copy.17
  (10 shorter events, 0.1 us)
Async XLA Ops:
  0.6 25.2 %copy-start = (bf16[3,256,1024]{2,1,0:T(8,128)(2,1)S(1)}, bf16[3,256,1024]{2,1,0:T(8,128)(2,1)}, u32[]{:S(2)}) copy-start(bf16[3,256,1024]{2,1,0:T(8,128)(2,1)} %param.13) | copy-start | bytes 4718596
  28.0 0.7 copy-start.7
  28.7 6.1 %copy-start.9 = (f32[3,256]{1,0:T(4,128)S(1)}, f32[3,256]{1,0:T(4,128)}, u32[]{:S(2)}) copy-start(f32[3,256]{1,0:T(4,128)} %param.15) | copy-start | bytes 9220
  28.7 12.0 %copy-start.3 = (s32[4,384]{1,0:T(4,128)S(1)}, s32[4,384]{1,0:T(4,128)}, u32[]{:S(2)}) copy-start(s32[4,384]{1,0:T(4,128)} %param.17) | copy-start | bytes 18436
  28.7 12.0 %copy-start.5 = (s32[3,512]{1,0:T(4,128)S(1)}, s32[3,512]{1,0:T(4,128)}, u32[]{:S(2)}) copy-start(s32[3,512]{1,0:T(4,128)} %param.16) | copy-start | bytes 18436
  29.1 12.5 %copy-start.6 = (f32[3,512]{1,0:T(4,128)S(1)}, f32[3,512]{1,0:T(4,128)}, u32[]{:S(2)}) copy-start(f32[3,512]{1,0:T(4,128)} %param.18) | copy-start | bytes 18436
  29.2 17.6 %collective-permute-start = (bf16[128,1536]{0,1:T(8,128)(2,1)S(1)}, bf16[128,1536]{0,1:T(8,128)(2,1)S(1)}, u32[]{:S(2)}, u32[]{:S(2)}) collective-permute-start(bf16[128,1536]{0,1:T(8,128)(2,1)S(1)} %get-tuple-element.56), channel_id=1, source_target_pairs={{0,2},{2,4},{4,6},{6,8},{8,10},{10,12},{12,14},{14,16},{16,18},{18... | collective-permute-start | bytes 1179656 | tf_op jit(solution)/shard_map/ppermute | solution.py:19
  29.7 17.1 %collective-permute-start.1 = (bf16[128,1536]{0,1:T(8,128)(2,1)S(1)}, bf16[128,1536]{0,1:T(8,128)(2,1)S(1)}, u32[]{:S(2)}, u32[]{:S(2)}) collective-permute-start(bf16[128,1536]{0,1:T(8,128)(2,1)S(1)} %get-tuple-element.57), channel_id=1, source_target_pairs={{0,30},{2,0},{4,2},{6,4},{8,6},{10,8},{12,10},{14,12},{16,14},{18,... | collective-permute-start | bytes 1179656 | tf_op jit(solution)/shard_map/ppermute | solution.py:19
  35.0 9.1 %collective-permute-start.2 = (f32[3,128]{1,0:T(4,128)S(1)}, f32[3,128]{1,0:T(4,128)S(1)}, u32[]{:S(2)}, u32[]{:S(2)}) collective-permute-start(f32[3,128]{1,0:T(4,128)S(1)} %get-tuple-element.76), channel_id=1, source_target_pairs={{0,2},{2,4},{4,6},{6,8},{8,10},{10,12},{12,14},{14,16},{16,18},{18... | collective-permute-start | bytes 4616 | tf_op jit(solution)/shard_map/ppermute | solution.py:19
  35.0 11.0 %collective-permute-start.3 = (f32[3,128]{1,0:T(4,128)S(1)}, f32[3,128]{1,0:T(4,128)S(1)}, u32[]{:S(2)}, u32[]{:S(2)}) collective-permute-start(f32[3,128]{1,0:T(4,128)S(1)} %get-tuple-element.77), channel_id=1, source_target_pairs={{0,30},{2,0},{4,2},{6,4},{8,6},{10,8},{12,10},{14,12},{16,14},{18,... | collective-permute-start | bytes 4616 | tf_op jit(solution)/shard_map/ppermute | solution.py:19
  46.1 0.7 copy-start.4
  56.7 6.6 %copy-start.1 = (bf16[1024,512]{1,0:T(8,128)(2,1)S(1)}, bf16[1024,512]{1,0:T(8,128)(2,1)}, u32[]{:S(2)}) copy-start(bf16[1024,512]{1,0:T(8,128)(2,1)} %shard_map.104) | copy-start | bytes 3145732
  56.8 6.6 %copy-start.8 = (f32[256]{0:T(256)S(1)}, f32[256]{0:T(256)}, u32[]{:S(2)}) copy-start(f32[256]{0:T(256)} %param.20) | copy-start | bytes 3076
  57.7 14.6 %collective-permute-start.4 = (bf16[128,1536]{1,0:T(8,128)(2,1)}, bf16[128,1536]{1,0:T(8,128)(2,1)S(1)}, u32[]{:S(2)}, u32[]{:S(2)}) collective-permute-start(bf16[128,1536]{1,0:T(8,128)(2,1)} %get-tuple-element.48), channel_id=1, source_target_pairs={{0,2},{2,4},{4,6},{6,8},{8,10},{10,12},{12,14},{14,16},{16,18},{18... | collective-permute-start | bytes 1179656 | tf_op jit(solution)/shard_map/ppermute | solution.py:19
  58.4 18.6 %collective-permute-start.5 = (bf16[128,1536]{1,0:T(8,128)(2,1)}, bf16[128,1536]{1,0:T(8,128)(2,1)S(1)}, u32[]{:S(2)}, u32[]{:S(2)}) collective-permute-start(bf16[128,1536]{1,0:T(8,128)(2,1)} %get-tuple-element.49), channel_id=1, source_target_pairs={{0,30},{2,0},{4,2},{6,4},{8,6},{10,8},{12,10},{14,12},{16,14},{18,... | collective-permute-start | bytes 1179656 | tf_op jit(solution)/shard_map/ppermute | solution.py:19
  63.3 40.5 %collective-permute-start.7 = (bf16[1024,512]{1,0:T(8,128)(2,1)S(1)}, bf16[1024,512]{1,0:T(8,128)(2,1)}, u32[]{:S(2)}, u32[]{:S(2)}) collective-permute-start(bf16[1024,512]{1,0:T(8,128)(2,1)S(1)} %copy-done.1), channel_id=1, source_target_pairs={{0,1},{1,0},{2,3},{3,2},{4,5},{5,4},{6,7},{7,6},{8,9},{9,8},{10,11... | collective-permute-start | bytes 3145736 | tf_op jit(solution)/shard_map/ppermute | solution.py:213
  79.8 22.9 %collective-permute-start.6 = (bf16[128,1536]{1,0:T(8,128)(2,1)}, bf16[128,1536]{1,0:T(8,128)(2,1)}, u32[]{:S(2)}, u32[]{:S(2)}) collective-permute-start(bf16[128,1536]{1,0:T(8,128)(2,1)} %constant_dynamic-slice_fusion.1), channel_id=1, source_target_pairs={{0,1},{1,0},{2,3},{3,2},{4,5},{5,4},{6,7},{7,6},{8,9},{9,8},{10,11... | collective-permute-start | bytes 1179656 | tf_op jit(solution)/shard_map/ppermute | solution.py:255
  105.6 1.4 %copy-start.2 = (f32[64,512]{1,0:T(8,128)S(1)}, f32[64,512]{1,0:T(8,128)}, u32[]{:S(2)}) copy-start(f32[64,512]{1,0:T(8,128)} %shard_map.105) | copy-start | bytes 393220

commit v2 on v1

--- a/solution.py
+++ b/solution.py
@@ -44,11 +44,13 @@
     return p, p // PLANE, p % PLANE, xnb, ynb
 
 
-def greet(peers):
+def greet(peers, pos=None):
     bar = pltpu.get_barrier_semaphore()
+    if pos is not None:
+        pl.semaphore_signal(bar, inc=1, device_id={"frame": 1 - pos}, device_id_type=MESH_ID)
     for q in peers:
         pl.semaphore_signal(bar, inc=1, device_id={"patch": q}, device_id_type=MESH_ID)
-    pl.semaphore_wait(bar, len(peers))
+    pl.semaphore_wait(bar, len(peers) + (pos is not None))
 
 
 def send(src, dst, ss, rs, q):
@@ -58,57 +60,96 @@
     )
 
 
-def gather_kernel(n, w, x_ref, o_ref, zs, zr, xs, xr, ys, yr, rs, rr):
+def gather_kernel(
+    n, w, hs, x_ref, b0, b1, b2, r_ref, o_ref, e0, e1, e2, t_ref,
+    zs, zr, xs, xr, ys, yr, rs, rr, hds, hdr, fs, fr, qs, qr
+):
     hi = n // PLANE
     p, h, lo, xnb, ynb = places(n)
-    lox, loy = xnb % PLANE, ynb % PLANE
+    pos = lax.axis_index("frame")
+    lox = xnb % PLANE
+    ring = [(p + n - 1) % n, (p + 1) % n]
+    bs, es = (b0, b1, b2), (e0, e1, e2)
 
     def rows(hh, ll):
         return o_ref.at[pl.ds(pl.multiple_of((hh * PLANE + ll) * w, w), w)]
 
+    def half(ref, d, which):
+        return ref.at[pl.ds(pl.multiple_of((2 * d + which) * hs, hs), hs)]
+
     zpeer = [((h + j) % hi) * PLANE + lo for j in range(hi)]
-    greet(zpeer[1:] + [xnb, ynb])
+    greet(zpeer[1:] + [xnb, ynb] + ring, pos)
     order = sorted(range(1, hi), key=lambda j: min(j, hi - j))
     mine = rows(h, lo)
     zc = {j: send(x_ref, mine, zs.at[j], zr.at[j], zpeer[j]) for j in order}
-    xc, yc, rc = {}, {}, {}
+    xc, yc, rc, hc, fc = {}, {}, {}, {}, {}
     xc[0] = send(x_ref, mine, xs.at[0], xr.at[0], xnb)
     yc[0] = send(x_ref, mine, ys.at[0], yr.at[0], ynb)
     xc[0].start()
     yc[0].start()
     for j in reversed(order):
         zc[j].start()
+    rest = [send(r_ref.at[d], t_ref.at[1 - d], qs.at[d], qr.at[d], ring[d]) for d in range(2)]
+    rest[0].start()
+    rest[1].start()
+
+    def halo(c):
+        for d in range(2):
+            hc[c, d] = send(
+                half(bs[c], d, pos), half(es[c], 1 - d, pos),
+                hds.at[2 * c + d], hdr.at[2 * c + d], ring[d],
+            )
+            hc[c, d].start()
+
+    def swap(c):
+        for d in range(2):
+            hc[c, d].wait_recv()
+            part = half(es[c], 1 - d, pos)
+            fc[c, d] = pltpu.make_async_remote_copy(
+                src_ref=part, dst_ref=part,
+                send_sem=fs.at[2 * c + d], recv_sem=fr.at[2 * c + d],
+                device_id={"frame": 1 - pos}, device_id_type=MESH_ID,
+            )
+            fc[c, d].start()
+
+    halo(0)
     mine[...] = x_ref[...]
 
     def relay(j):
-        hh = (h + hi - j) % hi
-        if j % 2 == 0:
-            xc[j].wait_recv()
-            part = rows(hh, lox)
-            rc[j] = send(part, part, rs.at[j], rr.at[j], ynb)
-        else:
-            yc[j].wait_recv()
-            part = rows(hh, loy)
-            rc[j] = send(part, part, rs.at[j], rr.at[j], xnb)
+        xc[j].wait_recv()
+        part = rows((h + hi - j) % hi, lox)
+        rc[j] = send(part, part, rs.at[j], rr.at[j], ynb)
         rc[j].start()
 
     last = 0
-    for j in order:
+    for at, j in enumerate(order):
         zc[j].wait_recv()
         part = rows((h + hi - j) % hi, lo)
         xc[j] = send(part, part, xs.at[j], xr.at[j], xnb)
         yc[j] = send(part, part, ys.at[j], yr.at[j], ynb)
         xc[j].start()
         yc[j].start()
+        if at == 1:
+            halo(1)
         relay(last)
         last = j
+    if len(order) < 2:
+        halo(1)
+    halo(2)
     relay(last)
+    for c in range(3):
+        swap(c)
     for j in range(hi):
-        if j % 2 == 0:
-            yc[j].wait_recv()
-        else:
-            xc[j].wait_recv()
+        yc[j].wait_recv()
         rc[j].wait_recv()
+    for d in range(2):
+        rest[d].wait_recv()
+        rest[d].wait_send()
+    for c in range(3):
+        for d in range(2):
+            fc[c, d].wait_recv()
+            fc[c, d].wait_send()
+            hc[c, d].wait_send()
     for j in range(hi):
         if j:
             zc[j].wait_send()
@@ -117,17 +158,21 @@
         rc[j].wait_send()
 
 
-def gather_all(x, n):
+def gather_all(x, bsend, rsend, n):
     w, f = x.shape
     hi = n // PLANE
+    slots, kk = bsend[0].shape
+    vm = pl.BlockSpec(memory_space=pltpu.VMEM)
     return pl.pallas_call(
-        functools.partial(gather_kernel, n, w),
-        out_shape=jax.ShapeDtypeStruct((n * w, f), x.dtype),
-        in_specs=[pl.BlockSpec(memory_space=pltpu.VMEM)],
-        out_specs=pl.BlockSpec(memory_space=pltpu.VMEM),
-        scratch_shapes=[DMA((hi,))] * 8,
+        functools.partial(gather_kernel, n, w, slots // 4),
+        out_shape=[jax.ShapeDtypeStruct((n * w, f), x.dtype)]
+        + [jax.ShapeDtypeStruct((slots, kk), x.dtype)] * 3
+        + [jax.ShapeDtypeStruct(rsend.shape, rsend.dtype)],
+        in_specs=[vm] * 5,
+        out_specs=[vm] * 5,
+        scratch_shapes=[DMA((hi,))] * 8 + [DMA((6,))] * 4 + [DMA((2,))] * 2,
         compiler_params=pltpu.CompilerParams(collective_id=0, has_side_effects=True),
-    )(x)
+    )(x, *bsend, rsend)
 
 
 def scatter_kernel(
@@ -209,8 +254,6 @@
     total = ff * lax.axis_size("frame")
     pos = lax.axis_index("frame")
     n = lax.axis_size("patch")
-    lat_t = gather_all(latents.T, n)
-    lat_o = lax.ppermute(lat_t, "frame", [(0, 1), (1, 0)])
     ext = vs + 2 * halo
     ta, tb, tc = (hot(ext, triangles[i]) for i in range(3))
     ha, hb, hc, hd = (hot(ext, hinges[i]) for i in range(4))
@@ -218,16 +261,18 @@
     self32 = hot(vs, send_rows.reshape(-1))
     sel = self32.astype(BF)
     rest_out = exact(rest_pos, self32)
-    rest_ext = jnp.concatenate(
-        [rest_pos, shift(rest_out[:, halo:], 1), shift(rest_out[:, :halo], -1)], axis=1
-    )
+    bsend = [mm(sel, basis[c], ((0,), (0,))).astype(BF) for c in range(3)]
+    rsend = jnp.pad(rest_out.reshape(3, 2, halo).transpose(1, 0, 2), ((0, 0), (0, 5), (0, 0)))
+    lat_t, *bhalo, rhalo = gather_all(latents.T, bsend, rsend, n)
+    lat_o = lax.ppermute(lat_t, "frame", [(0, 1), (1, 0)])
+    rest_ext = jnp.concatenate([rest_pos, rhalo[0, :3], rhalo[1, :3]], axis=1)
     rest_edge = exact(rest_ext, inc.astype(F32))
     rest_edge = rest_edge.at[:, 2 * nt :].add(-bend_rest)
     flat_basis = basis.reshape(3 * vs, kk)
     dec = mm(flat_basis, lat_t, ((1,), (0,))).astype(BF).reshape(3, vs, ff)
     own = jnp.concatenate([dec[0], dec[1], dec[2]], axis=1)
-    out = mm(sel, own, ((0,), (0,))).astype(BF)
-    dext = jnp.concatenate([own, shift(out[halo:], 1), shift(out[:halo], -1)], axis=0)
+    far = [mm(bhalo[c], lat_t, ((1,), (0,))).astype(BF) for c in range(3)]
+    dext = jnp.concatenate([own, jnp.concatenate(far, axis=1)], axis=0)
     edges = mm(inc, dext, ((0,), (0,)))
     e1 = [edges[:nt, c * ff : (c + 1) * ff] + rest_edge[c, :nt, None] for c in range(3)]
     e2 = [edges[nt : 2 * nt, c * ff : (c + 1) * ff] + rest_edge[c, nt : 2 * nt, None] for c in range(3)]

time: 108 us -> 112 us (1.037)
  starting transfers between devices: 17 us -> 5.63 us
  Pallas kernels: 45.3 us -> 53.9 us
  matrix products: 16.4 us -> 24.9 us
  waiting for transfers between devices: 18.1 us -> 16.7 us
    ppermute x6 -> x2, starting transfers between devices: 17 us -> 5.62 us  [shift(): return lax.ppermute(block, 'patch', [(i, (i + step) % n) for i in range(n)])]
    pallas_call x1, Pallas kernels: 25.1 us -> 34.5 us  [gather_all(): pl.pallas_call(functools.partial(gather_kernel, n, w, slots // 4), out_sh...]
    dot_general x8 -> x13, matrix products: 15.5 us -> 24.1 us  [mm(): return lax.dot_general(a, b, (dims, ((), ())), preferred_element_type=F32)]
    ppermute x6 -> x2, waiting for transfers between devices: 18.1 us -> 16.7 us  [shift(): return lax.ppermute(block, 'patch', [(i, (i + step) % n) for i in range(n)])]
  transfers between devices with their start and end apart: 8 -> 4, of which waited for: 4 -> 2; matrix products, arithmetic and copies ran while one was open for 8% -> 6% of each run, Pallas kernels for 19% -> 17%
where the time goes in v2:
time: 112 us
  Pallas kernels  53.9 us (48%)
  matrix products  24.9 us (22%)
  waiting for transfers between devices  16.7 us (15%)
  other arithmetic  5.67 us (5%)
  starting transfers between devices  5.63 us (5%)
  local copies, waits for them, and re-layouts  4.42 us (4%)
    pallas_call x1, Pallas kernels, gather_all(): pl.pallas_call(functools.partial(gather_kernel, n, w, slots // 4), out_sh...  34.5 us
    dot_general x13, matrix products, mm(): return lax.dot_general(a, b, (dims, ((), ())), preferred_element_type=F32)  24.1 us
    pallas_call x1, Pallas kernels, scatter_sum(): pl.pallas_call(functools.partial(scatter_kernel, n, w), out_shape=jax.Sha...  19.4 us
    ppermute x2, waiting for transfers between devices, shift(): return lax.ppermute(block, 'patch', [(i, (i + step) % n) for i in range(n)])  16.7 us
    ppermute x2, starting transfers between devices, shift(): return lax.ppermute(block, 'patch', [(i, (i + step) % n) for i in range(n)])  5.62 us
    another operation x6, other arithmetic  3.8 us
  transfers between devices with their start and end apart: 4, of which 2 were waited for; matrix products, arithmetic and copies ran while one was open for 6% of the time, Pallas kernels for 17%

profile of v2, /device:TPU:0, one launch (start us, length us, event | category | flops | bytes accessed | tf_op | source)
XLA Modules:
  0.0 112.2 jit_solution(7842659846712727200)
XLA Ops:
  0.6 0.0 copy-start.4
  0.6 0.0 copy-start.1
  0.7 0.0 copy-start.11
  0.7 2.3 %convolution_convert_fusion.4.b2 = bf16[256,1024]{1,0:T(8,128)(2,1)} fusion(bf16[3,256,1024]{2,1,0:T(8,128)(2,1)} %param.13, s32[256]{0:T(256)} %bitcast.69), kind=kOutput, calls=%fused_computation.38 | convolution fusion | flops 134676480 | bytes 1049600 | tf_op jit(solution)/shard_map/dot_general | solution.py:28
  3.0 2.2 %convolution_convert_fusion.5.b1 = bf16[256,1024]{1,0:T(8,128)(2,1)} fusion(bf16[3,256,1024]{2,1,0:T(8,128)(2,1)} %param.13, s32[256]{0:T(256)} %bitcast.70), kind=kOutput, calls=%fused_computation.39 | convolution fusion | flops 134676480 | bytes 1049600 | tf_op jit(solution)/shard_map/dot_general | solution.py:28
  5.2 0.0 copy-done.4
  5.2 0.0 copy-done.1
  5.2 1.1 convolution_convert_fusion.6.b0
  6.3 0.0 copy-done.11
  6.3 0.1 convolution_bitcast_fusion
  6.5 0.7 pad.8.r_ref
  7.1 34.5 %shard_map.104 = (bf16[1024,512]{1,0:T(8,128)(2,1)}, bf16[256,1024]{1,0:T(8,128)(2,1)}, bf16[256,1024]{1,0:T(8,128)(2,1)}, bf16[256,1024]{1,0:T(8,128)(2,1)}, f32[2,8,128]{2,1,0:T(8,128)}) custom-call(bf16[64,512]{1,0:T(8,128)(2,1)} %bitcast.56, bf16[256,1024]{1,0:T(8,128)(2,1)} %convolution_convert_fusion.6.b0, ...), custom_call_target="tpu_custom_call" | custom-call | tf_op jit(solution)/shard_map/pallas_call | solution.py:166
  41.6 0.0 copy-start
  41.6 0.0 copy-start.2
  41.6 2.0 %convolution_convert_fusion.9 = bf16[256,512]{0,1:T(8,128)(2,1)S(1)} fusion(bf16[256,1024]{1,0:T(8,128)(2,1)} %get-tuple-element.32, bf16[1024,512]{1,0:T(8,128)(2,1)} %get-tuple-element.31), kind=kOutput, calls=%fused_computation.44 | convolution fusion | flops 268566528 | bytes 1835008 | tf_op jit(solution)/shard_map/dot_general | solution.py:28
  43.6 1.9 %convolution_convert_fusion.8 = bf16[256,512]{0,1:T(8,128)(2,1)S(1)} fusion(bf16[256,1024]{1,0:T(8,128)(2,1)} %get-tuple-element.33, bf16[1024,512]{1,0:T(8,128)(2,1)} %get-tuple-element.31), kind=kOutput, calls=%fused_computation.43 | convolution fusion | flops 268566528 | bytes 1835008 | tf_op jit(solution)/shard_map/dot_general | solution.py:28
  45.6 0.0 copy-done
  45.6 0.0 copy-done.2
  45.6 0.5 convolution_convert_fusion.7
  46.1 0.0 copy-start.5
  46.1 0.0 copy-start.7
  46.1 0.0 copy-start.9
  46.2 1.0 fusion.28
  47.2 0.1 fusion.82
  47.3 0.0 copy-done.5
  47.3 0.0 copy-done.7
  47.3 0.0 copy-done.9
  47.3 0.4 fusion.29
  47.8 0.0 copy-start.8
  47.8 0.0 copy-start.6
  47.8 0.4 subtract_convert_fusion.6
  48.2 0.7 fusion.64
  48.9 0.0 copy-done.8
  48.9 0.0 copy-done.6
  49.0 2.5 %fusion.15 = f32[1408,1536]{1,0:T(8,128)S(1)} fusion(bf16[256,512]{0,1:T(8,128)(2,1)S(1)} %convolution_convert_fusion.7, bf16[256,512]{0,1:T(8,128)(2,1)S(1)} %convolution_convert_fusion.8, bf16[256,512]{0,1:T(8,128)(2,1)S(1)} %convolution_convert_fusion.9, bf16[256,512]{0,1:T(8,128)(2,1)S(1)} %get-tuple-element.67, ...), kind=kOutput, calls=%fused_computation.17 | convolution fusion | flops 2228355072 | bytes 11665408 | tf_op jit(solution)/shard_map/dot_general | solution.py:28
  51.4 1.3 %subtract_convert_fusion.5 = (bf16[512,512]{1,0:T(8,128)(2,1)S(1)}, f32[512,512]{1,0:T(8,128)S(1)}, f32[512,512]{1,0:T(8,128)S(1)}, f32[512,512]{1,0:T(8,128)S(1...) fusion(f32[1408,1536]{1,0:T(8,128)S(1)} %fusion.15, f32[512]{0:T(512)S(1)} %bitcast.74, f32[512]{0:T(512)S(1)} %bitcast.76, ...), kind=kLoop, calls=%fused_computation.62 | loop fusion | flops 7340032 | bytes 12075008 | tf_op jit(solution)/shard_map/convert.7
  52.7 0.6 subtract_convert_fusion.2
  53.3 0.2 slice_add_fusion.8
  53.6 0.1 fusion.14
  53.7 0.9 subtract_convert_fusion.4
  54.7 0.0 copy-start.10
  54.7 4.2 %fusion.87 = (bf16[512,1536]{1,0:T(8,128)(2,1)S(1)}, f32[512,1536]{1,0:T(8,128)}) fusion(bf16[384,1536]{1,0:T(8,128)(2,1)S(1)} %fusion.14, bf16[512,512]{1,0:T(8,128)(2,1)S(1)} %get-tuple-element.53, bf16[512,512]{1,0:T(8,128)(2,1)S(1)} %get-tuple-element.52, bf16[512,512]{1,0:T(8,128)(2,1)S(1)} %get-tuple-element.49, ...), kind=kOutput, calls=%fused_computation.146 | convolution fusion | flops 2249981952 | bytes 10485760 | tf_op jit(solution)/shard_map/dot_general | solution.py:28
  58.9 0.9 fusion.80
  59.9 1.7 %collective-permute-start = (bf16[128,1536]{1,0:T(8,128)(2,1)}, bf16[128,1536]{1,0:T(8,128)(2,1)S(1)}, u32[]{:S(2)}, u32[]{:S(2)}) collective-permute-start(bf16[128,1536]{1,0:T(8,128)(2,1)} %get-tuple-element.58), channel_id=1, source_target_pairs={{0,2},{2,4},{4,6},{6,8},{8,10},{10,12},{12,14},{14,16},{16,18},{18... | collective-permute-start | bytes 1179656 | tf_op jit(solution)/shard_map/ppermute | solution.py:19
  61.6 3.9 %collective-permute-start.1 = (bf16[128,1536]{1,0:T(8,128)(2,1)}, bf16[128,1536]{1,0:T(8,128)(2,1)S(1)}, u32[]{:S(2)}, u32[]{:S(2)}) collective-permute-start(bf16[128,1536]{1,0:T(8,128)(2,1)} %get-tuple-element.59), channel_id=1, source_target_pairs={{0,30},{2,0},{4,2},{6,4},{8,6},{10,8},{12,10},{14,12},{16,14},{18,... | collective-permute-start | bytes 1179656 | tf_op jit(solution)/shard_map/ppermute | solution.py:19
  65.5 0.0 collective-permute-start.3
  65.5 13.7 %collective-permute-done = bf16[128,1536]{1,0:T(8,128)(2,1)S(1)} collective-permute-done((bf16[128,1536]{1,0:T(8,128)(2,1)}, bf16[128,1536]{1,0:T(8,128)(2,1)S(1)}, u32[]{:S(2)}, u32[]{:S(2)}) %collective-permute-start) | collective-permute-done | bytes 393248 | tf_op jit(solution)/shard_map/ppermute | solution.py:19
  79.2 3.0 %collective-permute-done.1 = bf16[128,1536]{1,0:T(8,128)(2,1)S(1)} collective-permute-done((bf16[128,1536]{1,0:T(8,128)(2,1)}, bf16[128,1536]{1,0:T(8,128)(2,1)S(1)}, u32[]{:S(2)}, u32[]{:S(2)}) %collective-permute-start.1) | collective-permute-done | bytes 393248 | tf_op jit(solution)/shard_map/ppermute | solution.py:19
  82.2 1.8 %convolution_add_fusion = f32[256,1536]{1,0:T(8,128)S(1)} fusion(f32[512,1536]{1,0:T(8,128)} %get-tuple-element.89, bf16[128,1536]{1,0:T(8,128)(2,1)S(1)} %collective-permute-done.1, bf16[128,1536]{1,0:T(8,128)(2,1)S(1)} %collective-permute-done, s32[256]{0:T(256)S(1)} %bitcast.73), kind=kOutput, calls=%fused_computation.14 | convolution fusion | flops 203489280 | bytes 3933184 | tf_op jit(solution)/shard_map/dot_general | solution.py:28
  84.0 0.1 fusion.42
  84.1 0.1 convert_element_type.94
  84.2 0.1 fusion.81
  84.3 0.8 constant_dynamic-slice_fusion.1
  85.0 0.0 collective-permute-start.2
  85.0 2.0 %fusion.27.g_ref = bf16[1024,512]{1,0:T(8,128)(2,1)} fusion(bf16[768,1024]{1,0:T(8,128)(2,1)S(1)} %bitcast.53, bf16[256,512]{1,0:T(8,128)(2,1)S(1)} %get-tuple-element.61, bf16[256,512]{1,0:T(8,128)(2,1)S(1)} %get-tuple-element.62, bf16[256,512]{1,0:T(8,128)(2,1)S(1)} %get-tuple-element.60), kind=kOutput, calls=%fused_computation.37 | convolution fusion | flops 808189952 | bytes 3407872 | tf_op jit(solution)/shard_map/dot_general | solution.py:28
  87.0 19.4 %shard_map.105 = f32[64,512]{1,0:T(8,128)} custom-call(bf16[1024,512]{1,0:T(8,128)(2,1)} %fusion.27.g_ref), custom_call_target="tpu_custom_call" | custom-call | tf_op jit(solution)/shard_map/pallas_call | solution.py:238
  106.5 0.6 convolution_convert_fusion.2
  107.1 0.0 collective-permute-done.2
  107.1 1.1 fusion.83
  108.2 0.0 collective-permute-done.3
  108.2 1.8 %convolution_convert_fusion.1 = bf16[384,1024]{1,0:T(8,128)(2,1)S(1)} fusion(bf16[1024,512]{1,0:T(8,128)(2,1)} %collective-permute-done.3, bf16[128,512]{1,0:T(8,128)(2,1)S(1)} %get-tuple-element.70, bf16[128,512]{1,0:T(8,128)(2,1)S(1)} %get-tuple-element.71, bf16[128,512]{1,0:T(8,128)(2,1)S(1)} %get-tuple-element.69), kind=kOutput, calls=%fused_computation.34 | convolution fusion | flops 404226048 | bytes 2228224 | tf_op jit(solution)/shard_map/dot_general | solution.py:28
  110.1 0.0 copy-start.3
  110.1 1.4 %convert_add_fusion = f32[384,1024]{1,0:T(8,128)} fusion(bf16[384,1024]{1,0:T(8,128)(2,1)S(1)} %convolution_convert_fusion.1, bf16[384,1024]{1,0:T(8,128)(2,1)S(1)} %convolution_convert_fusion.2), kind=kLoop, calls=%fused_computation.29 | loop fusion | flops 1179648 | bytes 3145728 | tf_op jit(solution)/shard_map/add | solution.py:307
  111.5 0.7 copy.15
  (11 shorter events, 0.2 us)
Async XLA Ops:
  0.6 4.6 %copy-start.4 = (s32[2,128]{1,0:T(2,128)S(1)}, s32[2,128]{1,0:T(2,128)}, u32[]{:S(2)}) copy-start(s32[2,128]{1,0:T(2,128)} %param.21) | copy-start | bytes 3076
  0.6 4.6 %copy-start.1 = (bf16[3,256,1024]{2,1,0:T(8,128)(2,1)S(1)}, bf16[3,256,1024]{2,1,0:T(8,128)(2,1)}, u32[]{:S(2)}) copy-start(bf16[3,256,1024]{2,1,0:T(8,128)(2,1)} %param.13) | copy-start | bytes 4718596
  0.7 5.7 %copy-start.11 = (f32[3,256]{1,0:T(4,128)S(1)}, f32[3,256]{1,0:T(4,128)}, u32[]{:S(2)}) copy-start(f32[3,256]{1,0:T(4,128)} %param.15) | copy-start | bytes 9220
  41.6 4.0 %copy-start = (bf16[1024,512]{1,0:T(8,128)(2,1)S(1)}, bf16[1024,512]{1,0:T(8,128)(2,1)}, u32[]{:S(2)}) copy-start(bf16[1024,512]{1,0:T(8,128)(2,1)} %get-tuple-element.31) | copy-start | bytes 3145732
  41.6 4.0 %copy-start.2 = (bf16[256,1024]{1,0:T(8,128)(2,1)S(1)}, bf16[256,1024]{1,0:T(8,128)(2,1)}, u32[]{:S(2)}) copy-start(bf16[256,1024]{1,0:T(8,128)(2,1)} %get-tuple-element.34) | copy-start | bytes 1572868
  46.1 1.1 %copy-start.5 = (s32[4,384]{1,0:T(4,128)S(1)}, s32[4,384]{1,0:T(4,128)}, u32[]{:S(2)}) copy-start(s32[4,384]{1,0:T(4,128)} %param.17) | copy-start | bytes 18436
  46.1 1.2 %copy-start.7 = (s32[3,512]{1,0:T(4,128)S(1)}, s32[3,512]{1,0:T(4,128)}, u32[]{:S(2)}) copy-start(s32[3,512]{1,0:T(4,128)} %param.16) | copy-start | bytes 18436
  46.1 1.2 %copy-start.9 = (f32[2,8,128]{2,1,0:T(8,128)S(1)}, f32[2,8,128]{2,1,0:T(8,128)}, u32[]{:S(2)}) copy-start(f32[2,8,128]{2,1,0:T(8,128)} %get-tuple-element.35) | copy-start | bytes 24580
  47.8 1.1 copy-start.8
  47.8 1.1 %copy-start.6 = (f32[3,384]{1,0:T(4,128)S(1)}, f32[3,384]{1,0:T(4,128)}, u32[]{:S(2)}) copy-start(f32[3,384]{1,0:T(4,128)} %param.19) | copy-start | bytes 13828
  54.7 10.8 %copy-start.10 = (f32[256]{0:T(256)S(1)}, f32[256]{0:T(256)}, u32[]{:S(2)}) copy-start(f32[256]{0:T(256)} %param.20) | copy-start | bytes 3076
  59.9 19.3 %collective-permute-start = (bf16[128,1536]{1,0:T(8,128)(2,1)}, bf16[128,1536]{1,0:T(8,128)(2,1)S(1)}, u32[]{:S(2)}, u32[]{:S(2)}) collective-permute-start(bf16[128,1536]{1,0:T(8,128)(2,1)} %get-tuple-element.58), channel_id=1, source_target_pairs={{0,2},{2,4},{4,6},{6,8},{8,10},{10,12},{12,14},{14,16},{16,18},{18... | collective-permute-start | bytes 1179656 | tf_op jit(solution)/shard_map/ppermute | solution.py:19
  61.6 20.6 %collective-permute-start.1 = (bf16[128,1536]{1,0:T(8,128)(2,1)}, bf16[128,1536]{1,0:T(8,128)(2,1)S(1)}, u32[]{:S(2)}, u32[]{:S(2)}) collective-permute-start(bf16[128,1536]{1,0:T(8,128)(2,1)} %get-tuple-element.59), channel_id=1, source_target_pairs={{0,30},{2,0},{4,2},{6,4},{8,6},{10,8},{12,10},{14,12},{16,14},{18,... | collective-permute-start | bytes 1179656 | tf_op jit(solution)/shard_map/ppermute | solution.py:19
  65.5 42.7 %collective-permute-start.3 = (bf16[1024,512]{1,0:T(8,128)(2,1)S(1)}, bf16[1024,512]{1,0:T(8,128)(2,1)}, u32[]{:S(2)}, u32[]{:S(2)}) collective-permute-start(bf16[1024,512]{1,0:T(8,128)(2,1)S(1)} %copy-done), channel_id=1, source_target_pairs={{0,1},{1,0},{2,3},{3,2},{4,5},{5,4},{6,7},{7,6},{8,9},{9,8},{10,11... | collective-permute-start | bytes 3145736 | tf_op jit(solution)/shard_map/ppermute | solution.py:267
  85.0 22.1 %collective-permute-start.2 = (bf16[128,1536]{1,0:T(8,128)(2,1)}, bf16[128,1536]{1,0:T(8,128)(2,1)}, u32[]{:S(2)}, u32[]{:S(2)}) collective-permute-start(bf16[128,1536]{1,0:T(8,128)(2,1)} %constant_dynamic-slice_fusion.1), channel_id=1, source_target_pairs={{0,1},{1,0},{2,3},{3,2},{4,5},{5,4},{6,7},{7,6},{8,9},{9,8},{10,11... | collective-permute-start | bytes 1179656 | tf_op jit(solution)/shard_map/ppermute | solution.py:300
  110.1 1.4 %copy-start.3 = (f32[64,512]{1,0:T(8,128)S(1)}, f32[64,512]{1,0:T(8,128)}, u32[]{:S(2)}) copy-start(f32[64,512]{1,0:T(8,128)} %shard_map.105) | copy-start | bytes 393220
